TPU v7x, 128 devices: a whole 4x4x4 slice. The times are simulated.
128 devices in a mesh: bricks: 128 (over y, z, x, core).
Axes of the slice: x: 4, y: 4, z: 4, core: 2. Of those that a mesh axis runs over, the one named last changes fastest.
Arguments:
- calcium: float32 [256, 32, 1024], P('bricks'), may hold values from 0.2 to 1.5
- buffer: float32 [256, 32, 1024], P('bricks'), may hold values from 0.1 to 1.5
- fraction: float32 [256, 32, 1024], P('bricks'), may hold values from 0.1 to 0.4
- rates: float32 [256, 3, 2], P('bricks'), may hold values from 2 to 64
- inverses: float32 [256, 3, 2, 32, 32], P('bricks'), as said below
- neighbors: int32 [3, 2, 256], replicated, may hold values from -1 to 255, as said below
- ranks: int32 [3, 256], replicated, may hold values from 0 to 31, as said below
Outputs:
- calcium_next: float32 [256, 32, 1024], P('bricks')
- buffer_next: float32 [256, 32, 1024], P('bricks')
Inputs may be any that keep to these rules, and one draw needn't show every extreme that they name: neighbors[d, 0, s] and neighbors[d, 1, s] are the slots of the active bricks adjacent to slot s before and after it along dimension d of a block of 32 x 16 x 2 brick positions, -1 where that position is inactive or outside; active bricks fill whole rows along the first dimension. ranks[d, s] is the number of consecutive active bricks before slot s along dimension d. inverses[s, d, k] is the inverse of I + rates[s, d, k] K, K the 32 x 32 second difference with diagonal 1, 2, ..., 2, 1 and off-diagonals -1.
All inputs are finite; a program needn't handle non-finite values.
Results may differ from a plain program's by a relative error of at most 0.00015.
Values sent between devices are 32-bit elements; how exact they have to be, the bound alone decides.
A program may use at most 128 MiB of HBM per device.

v0:
```python
from functools import partial
import jax
import jax.numpy as jnp
from jax import lax
from jax.sharding import PartitionSpec as P

GX = 32
KON = 0.5
KOFF = 0.3
BTOT = 2.0
INFLUX = 0.1


def fetch(table, index):
    rows = jnp.take(table, jnp.maximum(index, 0), axis=0)
    has = (index >= 0).reshape((-1,) + (1,) * (rows.ndim - 1))
    return jnp.where(has, rows, jnp.zeros_like(rows))


def lookup(planes, before, after):
    sides = []
    for d in range(3):
        lower = fetch(planes[:, d, 1], before[d])
        upper = fetch(planes[:, d, 0], after[d])
        sides.append(jnp.stack([lower, upper], 1))
    return jnp.stack(sides, 1)


def coupling(rate_all, neighbors):
    per_dim = []
    for d in range(3):
        mine = rate_all[:, d]
        sides = []
        for side in range(2):
            other = fetch(mine, neighbors[d, side])
            has = (neighbors[d, side] >= 0)[:, None]
            sides.append(jnp.where(has, 2.0 * mine * other / (mine + other), jnp.zeros_like(mine)))
        per_dim.append(jnp.stack(sides, 1))
    return jnp.stack(per_dim, 1)


def end_planes(field):
    count, edge = (field.shape[0], field.shape[2])
    per_dim = []
    for d in range(3):
        first = lax.index_in_dim(field, 0, 2 + d, False).reshape(count, 2, edge * edge)
        last = lax.index_in_dim(field, edge - 1, 2 + d, False).reshape(count, 2, edge * edge)
        per_dim.append(jnp.stack([first, last], 1))
    return jnp.stack(per_dim, 1)


def operator(field, d, rate, glow, gup, hlow, hup):
    axis = 2 + d
    edge = field.shape[axis]
    plane_shape = lax.index_in_dim(field, 0, axis, False).shape
    lower_face = jnp.expand_dims(hlow.reshape(plane_shape), axis)
    upper_face = jnp.expand_dims(hup.reshape(plane_shape), axis)
    upper = jnp.concatenate([lax.slice_in_dim(field, 1, edge, axis=axis), upper_face], axis)
    lower = jnp.concatenate([lower_face, lax.slice_in_dim(field, 0, edge - 1, axis=axis)], axis)
    place = lax.broadcasted_iota(jnp.int32, field.shape, axis)
    inner = rate[:, :, None, None, None]
    c_up = jnp.where(place == edge - 1, gup[:, :, None, None, None], inner)
    c_down = jnp.where(place == 0, glow[:, :, None, None, None], inner)
    return c_up * (upper - field) + c_down * (lower - field)


def reaction(field, fraction):
    count, edge = (field.shape[0], field.shape[2])
    alpha = fraction.reshape(count, edge, edge, edge)
    calc, bound = (field[:, 0], field[:, 1])
    bind = KON * calc * (BTOT - bound) - KOFF * bound
    return jnp.stack([-bind + INFLUX * (1.0 - alpha) / alpha, bind], 1)


def apply_inverse(block, field, d):
    forms = ["psab,psbjk->psajk", "psab,psibk->psiak", "psab,psijb->psija"]
    return jnp.einsum(forms[d], block, field, precision=lax.Precision.HIGHEST)


def line_ends(field, d):
    count, edge = (field.shape[0], field.shape[2])
    first = lax.index_in_dim(field, 0, 2 + d, False).reshape(count, 2, edge * edge)
    last = lax.index_in_dim(field, edge - 1, 2 + d, False).reshape(count, 2, edge * edge)
    return jnp.stack([first, last], 2)


def block_terms(glow, gup, corner):
    v_first, v_last, w_first, w_last = (
        corner[..., 0],
        corner[..., 1],
        corner[..., 2],
        corner[..., 3],
    )
    a00 = 1.0 + glow * v_first
    a01 = gup * w_first
    a10 = glow * v_last
    a11 = 1.0 + gup * w_last
    lq0 = -glow * v_first
    lq1 = -glow * v_last
    up0 = -gup * w_first
    up1 = -gup * w_last
    return (a00, a01, a10, a11, lq0, lq1, up0, up1)


def chain_order(before, rank):
    slots = jnp.arange(before.shape[0], dtype=jnp.int32)
    pointer = jnp.where(before >= 0, before, slots)
    for step in range(GX.bit_length()):
        pointer = jnp.take(pointer, pointer, axis=0)
    sort_key = pointer * GX + rank
    order = jnp.argsort(sort_key)
    inverse_order = jnp.argsort(order)
    return (order, inverse_order)


def shift_down(values):
    return jnp.concatenate([jnp.zeros_like(values[:1]), values[:-1]], 0)


def shift_up(values):
    return jnp.concatenate([values[1:], jnp.zeros_like(values[:1])], 0)


def compose_maps(first_map, second_map):
    e00, e01, e10, e11 = first_map
    l00, l01, l10, l11 = second_map
    n00 = l00 * e00 + l01 * e10
    n01 = l00 * e01 + l01 * e11
    n10 = l10 * e00 + l11 * e10
    n11 = l10 * e01 + l11 * e11
    scale = jnp.abs(n00) + jnp.abs(n01) + jnp.abs(n10) + jnp.abs(n11)
    return (n00 / scale, n01 / scale, n10 / scale, n11 / scale)


def compose_affine(first_map, second_map):
    first_q, first_p = first_map
    second_q, second_p = second_map
    return (first_q * second_q, second_p + second_q * first_p)


def sorted_solve(glow, gup, corner, before, after, order, inverse_order, ends):
    glow = jnp.take(glow, order, axis=0)
    gup = jnp.take(gup, order, axis=0)
    corner = jnp.take(corner, order, axis=0)
    has_b = jnp.take(before, order, axis=0) >= 0
    has_a = jnp.take(after, order, axis=0) >= 0
    arranged = jnp.take(ends, order, axis=0)
    y0 = arranged[:, :, 0]
    y1 = arranged[:, :, 1]
    a00, a01, a10, a11, lq0, lq1, up0, up1 = block_terms(glow, gup, corner)
    maps = (
        -(lq0 * up1 - lq1 * up0),
        a00 * up1 - a10 * up0,
        -(lq0 * a11 - a01 * lq1),
        a00 * a11 - a01 * a10,
    )
    summed = lax.associative_scan(compose_maps, maps, axis=0)
    f1_prev = summed[1] / summed[3]
    fq = shift_down(f1_prev)
    b00 = a00 - lq0 * fq
    b10 = a10 - lq1 * fq
    det = b00 * a11 - a01 * b10
    f0 = (a11 * up0 - a01 * up1) / det
    f1 = (b00 * up1 - b10 * up0) / det
    slope = (-(b00 * lq1 - b10 * lq0) / det)[:, :, None]
    offset = (b00[:, :, None] * y1 - b10[:, :, None] * y0) / det[:, :, None]
    e1 = lax.associative_scan(compose_affine, (slope, offset), axis=0)[1]
    eq = shift_down(e1)
    e0 = (
        a11[:, :, None] * y0 - a01[:, :, None] * y1 - (a11 * lq0 - a01 * lq1)[:, :, None] * eq
    ) / det[:, :, None]
    zp = lax.associative_scan(compose_affine, (-f0[:, :, None], e0), reverse=True, axis=0)[1]
    pn = shift_up(zp)
    zq = e1 - f1[:, :, None] * pn
    low = jnp.where(has_b[:, None, None], zp - shift_down(zq), jnp.zeros_like(zp))
    high = jnp.where(has_a[:, None, None], zq - pn, jnp.zeros_like(zq))
    return jnp.take(jnp.stack([low, high], 2), inverse_order, axis=0)


def correct(local, block, glow, gup, jumps, d):
    axis = 2 + d
    count, edge = (local.shape[0], local.shape[2])
    shape_v = [count, 2, 1, 1, 1]
    shape_v[axis] = edge
    first_col = block[..., 0].reshape(shape_v)
    last_col = block[..., edge - 1].reshape(shape_v)
    plane_shape = lax.index_in_dim(local, 0, axis, False).shape
    low = jnp.expand_dims(jumps[:, :, 0].reshape(plane_shape), axis)
    high = jnp.expand_dims(jumps[:, :, 1].reshape(plane_shape), axis)
    return (
        local
        - glow[:, :, None, None, None] * low * first_col
        - gup[:, :, None, None, None] * high * last_col
    )


def body(calcium, buffer, fraction, rates, inverses, neighbors, ranks):
    count, edge = (calcium.shape[0], calcium.shape[1])
    devices = lax.axis_size("bricks")
    square = edge * edge
    per_device = square // devices
    start = lax.axis_index("bricks") * count
    corners = jnp.stack(
        [
            inverses[..., 0, 0],
            inverses[..., edge - 1, 0],
            inverses[..., 0, edge - 1],
            inverses[..., edge - 1, edge - 1],
        ],
        -1,
    )
    rate_all, corner_all = (
        lax.all_gather(rates, "bricks", axis=0, tiled=True),
        lax.all_gather(corners, "bricks", axis=0, tiled=True),
    )
    couple_all = coupling(rate_all, neighbors)
    couple = lax.dynamic_slice_in_dim(couple_all, start, count, 0)
    field = jnp.stack([calcium, buffer], 1).reshape(count, 2, edge, edge, edge)
    planes = end_planes(field).reshape(count, 3, 2, 2, devices, per_device)
    lined = lookup(
        lax.all_to_all(planes, "bricks", split_axis=4, concat_axis=0, tiled=True),
        neighbors[:, 0],
        neighbors[:, 1],
    )
    halos = lax.all_to_all(lined, "bricks", split_axis=0, concat_axis=4, tiled=True).reshape(
        count, 3, 2, 2, square
    )
    lams = [
        operator(
            field, d, rates[:, d], couple[:, d, 0], couple[:, d, 1], halos[:, d, 0], halos[:, d, 1]
        )
        for d in range(3)
    ]
    rhs = field + lams[0] + 2.0 * lams[1] + 2.0 * lams[2] + reaction(field, fraction)

    def solve(right, d):
        block = inverses[:, d]
        local = apply_inverse(block, right, d)
        ends = line_ends(local, d).reshape(count, 2, 2, devices, per_device)
        order, inverse_order = chain_order(neighbors[d, 0], ranks[d])
        chain_fn = partial(
            sorted_solve,
            couple_all[:, d, 0],
            couple_all[:, d, 1],
            corner_all[:, d],
            neighbors[d, 0],
            neighbors[d, 1],
            order,
            inverse_order,
        )
        lined_jumps = chain_fn(
            lax.all_to_all(ends, "bricks", split_axis=3, concat_axis=0, tiled=True)[:, :, :, 0]
        )[:, :, :, None]
        jumps = lax.all_to_all(
            lined_jumps, "bricks", split_axis=0, concat_axis=3, tiled=True
        ).reshape(count, 2, 2, square)
        return correct(local, block, couple[:, d, 0], couple[:, d, 1], jumps, d)

    first = solve(rhs, 0)
    second = solve(first - lams[1], 1)
    third = solve(second - lams[2], 2)
    result = third.reshape(count, 2, edge, edge * edge)
    return (result[:, 0], result[:, 1])


def solution(mesh):
    in_specs = (
        P("bricks", None, None),
        P("bricks", None, None),
        P("bricks", None, None),
        P("bricks", None, None),
        P("bricks", None, None, None, None),
        P(),
        P(),
    )
    out_specs = (P("bricks", None, None), P("bricks", None, None))
    return jax.shard_map(body, mesh=mesh, in_specs=in_specs, out_specs=out_specs, check_vma=False)
```

profile of v0, /device:TPU:1, one launch (start us, length us, event | category | flops | bytes accessed | tf_op | source)
XLA Modules:
  0.0 658.5 jit_solution(8018914261589705422)
XLA Ops:
  2.0 2.3 reshape.397
  5.6 5.8 divide_add_fusion
  12.0 2.8 fusion.206
  15.2 2.6 copy.2438
  18.0 2.6 copy.2439
  21.8 2.1 copy.2442
  23.9 4.2 reshape.1049
  28.1 12.3 %all-to-all-start = ((f32[128,1,192]{2,1,0:T(1,128)}), f32[128,1,192]{2,1,0:T(1,128)}, u32[]{:S(2)}, u32[]{:S(2)}) async-start(f32[128,1,192]{2,1,0:T(1,128)} %reshape.1049), calls=%async_computation | async-start | bytes 262144 | tf_op jit(solution)/shard_map/all_to_all | solution.py:221
  40.5 1.9 gather_fusion.38
  44.5 1.9 gather_fusion.40
  46.4 1.9 gather_fusion.41
  53.0 3.2 sort.91
  56.2 3.2 sort.92
  63.8 38.2 %all_gather.7 = f32[256,3,2,4]{1,2,0,3:T(2,128)S(1)} all-gather(f32[2,3,2,4]{1,2,0,3:T(2,128)S(1)} %pad_maximum_fusion.7), channel_id=1, replica_groups=mesh['bricks'=128] {'bricks'}, dimensions={0}, use_global_device_ids=true | all-gather | bytes 24768 | tf_op jit(solution)/shard_map/all_gather | solution.py:214
  102.1 3.6 fusion.208
  107.9 2.6 gather_fusion.46
  114.2 33.5 %all_gather.6 = f32[256,3,2]{1,2,0:T(2,128)S(1)} all-gather(f32[2,3,2]{1,2,0:T(2,128)S(1)} %copy-done.20), channel_id=1, replica_groups=mesh['bricks'=128] {'bricks'}, dimensions={0}, use_global_device_ids=true | all-gather | bytes 6192 | tf_op jit(solution)/shard_map/all_gather | solution.py:213
  149.1 2.5 copy.2539
  191.8 1.9 gather_fusion.28
  193.8 1.9 gather_fusion.29
  197.8 3.2 sort.89
  201.0 3.2 sort.90
  212.0 2.6 copy.2538
  250.9 1.9 gather_fusion.13
  252.9 1.9 gather_fusion.14
  260.9 3.2 sort.87
  264.1 3.2 sort.88
  272.3 2.6 copy.2537
  307.0 3.2 fusion.204
  311.0 2.4 fusion.202
  313.5 2.6 fusion.203
  338.7 3.2 reshape.1050
  341.9 1.9 bitcast_bitcast_fusion
  346.0 1.9 gather_fusion.6
  348.0 2.1 fusion.51
  352.1 2.1 fusion.49
  356.6 2.1 fusion.47
  358.6 2.1 gather_fusion.9
  360.8 2.1 fusion.45
  364.1 2.1 gather_fusion.10
  366.2 2.2 fusion.43
  368.5 2.1 gather_fusion.11
  374.5 4.2 reshape.1051
  378.8 5.8 all-to-all-start.1
  384.6 9.9 %all-to-all-done.1 = f32[128,1,192]{2,1,0:T(1,128)S(1)} async-done(((f32[128,1,192]{2,1,0:T(1,128)}), f32[128,1,192]{2,1,0:T(1,128)S(1)}, u32[]{:S(2)}, u32[]{:S(2)}) %all-to-all-start.1) | async-done | bytes 98336 | tf_op jit(solution)/shard_map/all_to_all | solution.py:225
  395.5 3.2 reshape.1052
  401.6 2.2 reshape.396
  403.9 2.9 copy.2458
  406.9 2.9 copy.2460
  410.5 4.8 fusion.18
  417.5 3.8 fusion.31
  424.3 4.2 all-to-all-start.2
  477.1 9.7 %all-to-all-start.3 = ((f32[256,2,2,1,8]{4,2,1,3,0:T(2,128)}), f32[256,2,2,1,8]{4,2,1,3,0:T(2,128)S(1)}, u32[]{:S(2)}, u32[]{:S(2)}) async-start(f32[256,2,2,1,8]{4,2,1,3,0:T(2,128)} %select_bitcast_fusion.2), calls=%async_computation.3 | async-start | bytes 1048576 | tf_op jit(solution)/shard_map/all_to_all | solution.py:254
  487.7 12.5 %all-to-all-done.3 = f32[256,2,2,1,8]{4,2,1,3,0:T(2,128)S(1)} async-done(((f32[256,2,2,1,8]{4,2,1,3,0:T(2,128)}), f32[256,2,2,1,8]{4,2,1,3,0:T(2,128)S(1)}, u32[]{:S(2)}, u32[]{:S(2)}) %all-to-all-start.3) | async-done | bytes 32800 | tf_op jit(solution)/shard_map/all_to_all | solution.py:254
  501.2 3.7 subtract_subtract_fusion.1
  504.9 3.2 fusion.25
  511.0 4.9 all-to-all-start.4
  556.6 9.6 %all-to-all-start.5 = ((f32[256,2,2,1,8]{4,1,2,3,0:T(2,128)}), f32[256,2,2,1,8]{4,1,2,3,0:T(2,128)S(1)}, u32[]{:S(2)}, u32[]{:S(2)}) async-start(f32[256,2,2,1,8]{4,1,2,3,0:T(2,128)} %copy.2505), calls=%async_computation.5 | async-start | bytes 1048576 | tf_op jit(solution)/shard_map/all_to_all | solution.py:254
  566.6 13.1 %all-to-all-done.5 = f32[256,2,2,1,8]{4,1,2,3,0:T(2,128)S(1)} async-done(((f32[256,2,2,1,8]{4,1,2,3,0:T(2,128)}), f32[256,2,2,1,8]{4,1,2,3,0:T(2,128)S(1)}, u32[]{:S(2)}, u32[]{:S(2)}) %all-to-all-start.5) | async-done | bytes 32800 | tf_op jit(solution)/shard_map/all_to_all | solution.py:254
  580.5 3.7 subtract_subtract_fusion
  584.3 9.1 %fusion.23 = f32[2,2,32,32,32]{3,4,2,1,0:T(8,128)S(1)} fusion(f32[2,2,32,32,32]{4,2,3,1,0:T(8,128)S(1)} %subtract_subtract_fusion, f32[2,3,2,32,32]{4,3,2,1,0:T(8,128)S(1)} %copy-done.18), kind=kOutput, calls=%fused_computation.78 | convolution fusion | flops 50331648 | bytes 2686976 | tf_op jit(solution)/shard_map/psab,psijb->psija/dot_general | solution.py:77
  595.3 4.9 all-to-all-start.6
  602.2 11.5 %all-to-all-done.6 = f32[2,2,2,128,8]{4,1,0,2,3:T(2,128)S(1)} async-done(((f32[2,2,2,128,8]{4,1,0,2,3:T(2,128)}), f32[2,2,2,128,8]{4,1,0,2,3:T(2,128)S(1)}, u32[]{:S(2)}, u32[]{:S(2)}) %all-to-all-start.6) | async-done | bytes 32800 | tf_op jit(solution)/shard_map/all_to_all | solution.py:252
  633.6 18.0 %all_to_all.123 = f32[256,2,2,1,8]{4,1,2,3,0:T(2,128)S(1)} all-to-all(f32[256,2,2,1,8]{4,1,2,3,0:T(2,128)S(1)} %copy.2524), channel_id=1, replica_groups=mesh['bricks'=128] {'bricks'}, dimensions={0} | all-to-all | bytes 65536 | tf_op jit(solution)/shard_map/all_to_all | solution.py:254
  (2082 shorter events, 317.5 us)
Async XLA Ops:
  21.6 18.8 %copy-start.187 = (s32[3,2,256]{2,1,0:T(2,128)S(1)}, s32[3,2,256]{2,1,0:T(2,128)}, u32[]{:S(2)}) copy-start(s32[3,2,256]{2,1,0:T(2,128)} %param.22) | copy-start | bytes 18436
  28.1 308.1 %all-to-all-start = ((f32[128,1,192]{2,1,0:T(1,128)}), f32[128,1,192]{2,1,0:T(1,128)}, u32[]{:S(2)}, u32[]{:S(2)}) async-start(f32[128,1,192]{2,1,0:T(1,128)} %reshape.1049), calls=%async_computation | async-start | bytes 262144 | tf_op jit(solution)/shard_map/all_to_all | solution.py:221
  187.1 30.3 %copy-start.196 = (pred[256]{0:T(512)(128)(4,1)}, pred[256]{0:T(512)(128)(4,1)S(1)}, u32[]{:S(2)}) copy-start(pred[256]{0:T(512)(128)(4,1)S(1)} %get-tuple-element.622) | copy-start | bytes 772
  187.1 30.3 %copy-start.198 = (pred[256]{0:T(512)(128)(4,1)}, pred[256]{0:T(512)(128)(4,1)S(1)}, u32[]{:S(2)}) copy-start(pred[256]{0:T(512)(128)(4,1)S(1)} %get-tuple-element.623) | copy-start | bytes 772
  187.1 30.3 %copy-start.200 = (pred[256]{0:T(512)(128)(4,1)}, pred[256]{0:T(512)(128)(4,1)S(1)}, u32[]{:S(2)}) copy-start(pred[256]{0:T(512)(128)(4,1)S(1)} %get-tuple-element.646) | copy-start | bytes 772
  187.2 30.3 %copy-start.202 = (pred[256]{0:T(512)(128)(4,1)}, pred[256]{0:T(512)(128)(4,1)S(1)}, u32[]{:S(2)}) copy-start(pred[256]{0:T(512)(128)(4,1)S(1)} %get-tuple-element.647) | copy-start | bytes 772
  195.8 18.7 %copy-start.240 = (s32[256]{0:T(256)S(1)}, s32[256]{0:T(256)}, u32[]{:S(2)}) copy-start(s32[256]{0:T(256)} %get-tuple-element.643) | copy-start | bytes 3076
  248.8 27.4 %copy-start.204 = (pred[256]{0:T(512)(128)(4,1)}, pred[256]{0:T(512)(128)(4,1)S(1)}, u32[]{:S(2)}) copy-start(pred[256]{0:T(512)(128)(4,1)S(1)} %get-tuple-element.618) | copy-start | bytes 772
  248.9 27.4 %copy-start.206 = (pred[256]{0:T(512)(128)(4,1)}, pred[256]{0:T(512)(128)(4,1)S(1)}, u32[]{:S(2)}) copy-start(pred[256]{0:T(512)(128)(4,1)S(1)} %get-tuple-element.619) | copy-start | bytes 772
  248.9 27.4 %copy-start.208 = (pred[256]{0:T(512)(128)(4,1)}, pred[256]{0:T(512)(128)(4,1)S(1)}, u32[]{:S(2)}) copy-start(pred[256]{0:T(512)(128)(4,1)S(1)} %get-tuple-element.648) | copy-start | bytes 772
  248.9 27.4 %copy-start.210 = (pred[256]{0:T(512)(128)(4,1)}, pred[256]{0:T(512)(128)(4,1)S(1)}, u32[]{:S(2)}) copy-start(pred[256]{0:T(512)(128)(4,1)S(1)} %get-tuple-element.649) | copy-start | bytes 772
  276.6 30.2 %copy-start.7 = (f32[256,1,2,2]{3,0,2,1:T(8,128)S(1)}, f32[256,1,2,2]{3,0,2,1:T(8,128)}, u32[]{:S(2)}) copy-start(f32[256,1,2,2]{3,0,2,1:T(8,128)} %copy-done.6) | copy-start | bytes 12292
  276.6 30.3 %copy-start.5 = (f32[256,1,2,2]{3,0,2,1:T(8,128)S(1)}, f32[256,1,2,2]{3,0,2,1:T(8,128)}, u32[]{:S(2)}) copy-start(f32[256,1,2,2]{3,0,2,1:T(8,128)} %copy-done.4) | copy-start | bytes 12292
  302.8 31.3 %copy-start.126 = (f32[2,2,1]{0,1,2:T(2,128)}, f32[2,2,1]{0,1,2:T(2,128)S(1)}, u32[]{:S(2)}) copy-start(f32[2,2,1]{0,1,2:T(2,128)S(1)} %slice.3220) | copy-start | bytes 52
  306.6 27.6 %copy-start.159 = (f32[2,2,1]{0,1,2:T(2,128)}, f32[2,2,1]{0,1,2:T(2,128)S(1)}, u32[]{:S(2)}) copy-start(f32[2,2,1]{0,1,2:T(2,128)S(1)} %slice.3154) | copy-start | bytes 52
  327.9 82.4 %copy-start.88 = (f32[2,1,1,2]{3,0,2,1:T(2,128)}, f32[2,1,1,2]{3,0,2,1:T(2,128)S(1)}, u32[]{:S(2)}) copy-start(f32[2,1,1,2]{3,0,2,1:T(2,128)S(1)} %copy.2457) | copy-start | bytes 52
  328.0 82.4 %copy-start.90 = (f32[2,1,1,2]{3,0,2,1:T(2,128)}, f32[2,1,1,2]{3,0,2,1:T(2,128)S(1)}, u32[]{:S(2)}) copy-start(f32[2,1,1,2]{3,0,2,1:T(2,128)S(1)} %copy.2459) | copy-start | bytes 52
  328.0 87.2 %copy-start.92 = (f32[2,1,1,2]{3,0,2,1:T(2,128)}, f32[2,1,1,2]{3,0,2,1:T(2,128)S(1)}, u32[]{:S(2)}) copy-start(f32[2,1,1,2]{3,0,2,1:T(2,128)S(1)} %copy.2455) | copy-start | bytes 52
  378.8 15.8 %all-to-all-start.1 = ((f32[128,1,192]{2,1,0:T(1,128)}), f32[128,1,192]{2,1,0:T(1,128)S(1)}, u32[]{:S(2)}, u32[]{:S(2)}) async-start(f32[128,1,192]{2,1,0:T(1,128)} %reshape.1051), calls=%async_computation.1 | async-start | bytes 262144 | tf_op jit(solution)/shard_map/all_to_all | solution.py:225
  384.6 30.7 %copy-start.244 = (pred[32]{0:T(512)(128)(4,1)}, pred[32]{0:T(512)(128)(4,1)S(1)}, u32[]{:S(2)}) copy-start(pred[32]{0:T(512)(128)(4,1)S(1)} %get-tuple-element.654) | copy-start | bytes 100
  384.6 30.7 %copy-start.246 = (pred[32]{0:T(512)(128)(4,1)}, pred[32]{0:T(512)(128)(4,1)S(1)}, u32[]{:S(2)}) copy-start(pred[32]{0:T(512)(128)(4,1)S(1)} %get-tuple-element.655) | copy-start | bytes 100
  424.3 17.9 %all-to-all-start.2 = ((f32[2,2,2,128,8]{4,1,0,2,3:T(2,128)}), f32[2,2,2,128,8]{4,1,0,2,3:T(2,128)S(1)}, u32[]{:S(2)}, u32[]{:S(2)}) async-start(f32[2,2,2,128,8]{4,1,0,2,3:T(2,128)} %copy.2475), calls=%async_computation.2 | async-start | bytes 1048576 | tf_op jit(solution)/shard_map/all_to_all | solution.py:252
  444.1 23.5 %copy-start.129 = (f32[4,2,1]{0,1,2:T(2,128)S(1)}, f32[4,2,1]{0,1,2:T(2,128)}, u32[]{:S(2)}) copy-start(f32[4,2,1]{0,1,2:T(2,128)} %copy-done.128) | copy-start | bytes 100
  444.1 24.7 %copy-start.127 = (f32[2,2,1]{0,1,2:T(2,128)S(1)}, f32[2,2,1]{0,1,2:T(2,128)}, u32[]{:S(2)}) copy-start(f32[2,2,1]{0,1,2:T(2,128)} %copy-done.126) | copy-start | bytes 52
  444.1 24.7 %copy-start.265 = (f32[2]{0:T(128)S(1)}, f32[2]{0:T(128)}, u32[]{:S(2)}) copy-start(f32[2]{0:T(128)} %slice_reduce_fusion.29) | copy-start | bytes 28
  444.2 24.9 %copy-start.264 = (f32[2]{0:T(128)S(1)}, f32[2]{0:T(128)}, u32[]{:S(2)}) copy-start(f32[2]{0:T(128)} %slice_reduce_fusion.30) | copy-start | bytes 28
  444.2 25.5 %copy-start.231 = (f32[3,2,1]{0,1,2:T(2,128)S(1)}, f32[3,2,1]{0,1,2:T(2,128)}, u32[]{:S(2)}) copy-start(f32[3,2,1]{0,1,2:T(2,128)} %slice.3211) | copy-start | bytes 76
  444.2 25.7 %copy-start.229 = (f32[7,2,1]{0,1,2:T(2,128)S(1)}, f32[7,2,1]{0,1,2:T(2,128)}, u32[]{:S(2)}) copy-start(f32[7,2,1]{0,1,2:T(2,128)} %slice.3204) | copy-start | bytes 172
  444.2 26.3 %copy-start.227 = (f32[15,2,1]{0,1,2:T(2,128)S(1)}, f32[15,2,1]{0,1,2:T(2,128)}, u32[]{:S(2)}) copy-start(f32[15,2,1]{0,1,2:T(2,128)} %slice.3197) | copy-start | bytes 364
  444.2 26.5 %copy-start.225 = (f32[31,2,1]{0,1,2:T(2,128)S(1)}, f32[31,2,1]{0,1,2:T(2,128)}, u32[]{:S(2)}) copy-start(f32[31,2,1]{0,1,2:T(2,128)} %slice.3190) | copy-start | bytes 748
  444.2 27.3 %copy-start.223 = (f32[63,2,1]{0,1,2:T(2,128)S(1)}, f32[63,2,1]{0,1,2:T(2,128)}, u32[]{:S(2)}) copy-start(f32[63,2,1]{0,1,2:T(2,128)} %slice.3183) | copy-start | bytes 1516
  444.2 27.8 %copy-start.221 = (f32[127,2,1]{0,1,2:T(2,128)S(1)}, f32[127,2,1]{0,1,2:T(2,128)}, u32[]{:S(2)}) copy-start(f32[127,2,1]{0,1,2:T(2,128)} %slice.3172) | copy-start | bytes 3052
  444.2 29.1 %copy-start.186 = (f32[256,2]{0,1:T(2,128)S(1)}, f32[256,2]{0,1:T(2,128)}, u32[]{:S(2)}) copy-start(f32[256,2]{0,1:T(2,128)} %get-tuple-element.248) | copy-start | bytes 6148
  444.2 29.1 %copy-start.255 = (pred[256]{0:T(512)(128)(4,1)S(1)}, pred[256]{0:T(512)(128)(4,1)}, u32[]{:S(2)}) copy-start(pred[256]{0:T(512)(128)(4,1)} %select_compare_fusion.4) | copy-start | bytes 772
  444.2 29.1 %copy-start.252 = (pred[256]{0:T(512)(128)(4,1)S(1)}, pred[256]{0:T(512)(128)(4,1)}, u32[]{:S(2)}) copy-start(pred[256]{0:T(512)(128)(4,1)} %get-tuple-element.244) | copy-start | bytes 772
  477.0 23.8 %copy-start.218 = (f32[2,1,1,2]{3,0,2,1:T(2,128)S(1)}, f32[2,1,1,2]{3,0,2,1:T(2,128)}, u32[]{:S(2)}) copy-start(f32[2,1,1,2]{3,0,2,1:T(2,128)} %copy.2454) | copy-start | bytes 52
  477.0 24.0 %copy-start.216 = (f32[2,1,1,2]{3,0,2,1:T(2,128)S(1)}, f32[2,1,1,2]{3,0,2,1:T(2,128)}, u32[]{:S(2)}) copy-start(f32[2,1,1,2]{3,0,2,1:T(2,128)} %copy.2433) | copy-start | bytes 52
  477.0 24.1 %copy-start.93 = (f32[2,1,1,2]{3,0,2,1:T(2,128)S(1)}, f32[2,1,1,2]{3,0,2,1:T(2,128)}, u32[]{:S(2)}) copy-start(f32[2,1,1,2]{3,0,2,1:T(2,128)} %copy-done.92) | copy-start | bytes 52
  477.0 24.1 %copy-start.96 = (f32[2,1,1,2]{3,0,2,1:T(2,128)S(1)}, f32[2,1,1,2]{3,0,2,1:T(2,128)}, u32[]{:S(2)}) copy-start(f32[2,1,1,2]{3,0,2,1:T(2,128)} %copy.2456) | copy-start | bytes 52
  477.0 24.1 %copy-start.181 = (f32[2,2,32]{2,1,0:T(2,128)S(1)}, f32[2,2,32]{2,1,0:T(2,128)}, u32[]{:S(2)}) copy-start(f32[2,2,32]{2,1,0:T(2,128)} %get-tuple-element.29) | copy-start | bytes 1540
  477.0 24.1 %copy-start.182 = (f32[2,2,32]{2,1,0:T(2,128)S(1)}, f32[2,2,32]{2,1,0:T(2,128)}, u32[]{:S(2)}) copy-start(f32[2,2,32]{2,1,0:T(2,128)} %get-tuple-element.30) | copy-start | bytes 1540
  477.0 24.1 %copy-start.213 = (f32[2,2]{1,0:T(2,128)S(1)}, f32[2,2]{1,0:T(2,128)}, u32[]{:S(2)}) copy-start(f32[2,2]{1,0:T(2,128)} %get-tuple-element.37) | copy-start | bytes 52
  477.0 24.1 %copy-start.245 = (pred[32]{0:T(512)(128)(4,1)S(1)}, pred[32]{0:T(512)(128)(4,1)}, u32[]{:S(2)}) copy-start(pred[32]{0:T(512)(128)(4,1)} %copy-done.244) | copy-start | bytes 100
  477.1 24.1 %copy-start.247 = (pred[32]{0:T(512)(128)(4,1)S(1)}, pred[32]{0:T(512)(128)(4,1)}, u32[]{:S(2)}) copy-start(pred[32]{0:T(512)(128)(4,1)} %copy-done.246) | copy-start | bytes 100
  477.1 23.2 %all-to-all-start.3 = ((f32[256,2,2,1,8]{4,2,1,3,0:T(2,128)}), f32[256,2,2,1,8]{4,2,1,3,0:T(2,128)S(1)}, u32[]{:S(2)}, u32[]{:S(2)}) async-start(f32[256,2,2,1,8]{4,2,1,3,0:T(2,128)} %select_bitcast_fusion.2), calls=%async_computation.3 | async-start | bytes 1048576 | tf_op jit(solution)/shard_map/all_to_all | solution.py:254
  511.0 18.4 %all-to-all-start.4 = ((f32[2,2,2,128,8]{4,1,0,2,3:T(2,128)}), f32[2,2,2,128,8]{4,1,0,2,3:T(2,128)S(1)}, u32[]{:S(2)}, u32[]{:S(2)}) async-start(f32[2,2,2,128,8]{4,1,0,2,3:T(2,128)} %copy.2495), calls=%async_computation.4 | async-start | bytes 1048576 | tf_op jit(solution)/shard_map/all_to_all | solution.py:252
  530.1 18.7 %copy-start.113 = (f32[2,2,1]{0,1,2:T(2,128)S(1)}, f32[2,2,1]{0,1,2:T(2,128)}, u32[]{:S(2)}) copy-start(f32[2,2,1]{0,1,2:T(2,128)} %slice.3512) | copy-start | bytes 52
  531.4 19.0 %copy-start.228 = (f32[15,2,1]{0,1,2:T(2,128)S(1)}, f32[15,2,1]{0,1,2:T(2,128)}, u32[]{:S(2)}) copy-start(f32[15,2,1]{0,1,2:T(2,128)} %slice.3489) | copy-start | bytes 364
  531.4 19.3 %copy-start.226 = (f32[31,2,1]{0,1,2:T(2,128)S(1)}, f32[31,2,1]{0,1,2:T(2,128)}, u32[]{:S(2)}) copy-start(f32[31,2,1]{0,1,2:T(2,128)} %slice.3482) | copy-start | bytes 748
  531.4 20.1 %copy-start.224 = (f32[63,2,1]{0,1,2:T(2,128)S(1)}, f32[63,2,1]{0,1,2:T(2,128)}, u32[]{:S(2)}) copy-start(f32[63,2,1]{0,1,2:T(2,128)} %slice.3475) | copy-start | bytes 1516
  531.4 20.6 %copy-start.222 = (f32[127,2,1]{0,1,2:T(2,128)S(1)}, f32[127,2,1]{0,1,2:T(2,128)}, u32[]{:S(2)}) copy-start(f32[127,2,1]{0,1,2:T(2,128)} %slice.3464) | copy-start | bytes 3052
  531.4 21.9 %copy-start.185 = (f32[256,2]{0,1:T(2,128)S(1)}, f32[256,2]{0,1:T(2,128)}, u32[]{:S(2)}) copy-start(f32[256,2]{0,1:T(2,128)} %get-tuple-element.146) | copy-start | bytes 6148
  531.4 21.9 %copy-start.254 = (pred[256]{0:T(512)(128)(4,1)S(1)}, pred[256]{0:T(512)(128)(4,1)}, u32[]{:S(2)}) copy-start(pred[256]{0:T(512)(128)(4,1)} %select_compare_fusion.2) | copy-start | bytes 772
  531.5 21.9 %copy-start.249 = (pred[256]{0:T(512)(128)(4,1)S(1)}, pred[256]{0:T(512)(128)(4,1)}, u32[]{:S(2)}) copy-start(pred[256]{0:T(512)(128)(4,1)} %get-tuple-element.142) | copy-start | bytes 772
  556.6 23.7 %copy-start.97 = (f32[2,1,1,2]{3,0,2,1:T(2,128)S(1)}, f32[2,1,1,2]{3,0,2,1:T(2,128)}, u32[]{:S(2)}) copy-start(f32[2,1,1,2]{3,0,2,1:T(2,128)} %copy.2456) | copy-start | bytes 52
  556.6 23.9 %copy-start.94 = (f32[2,1,1,2]{3,0,2,1:T(2,128)S(1)}, f32[2,1,1,2]{3,0,2,1:T(2,128)}, u32[]{:S(2)}) copy-start(f32[2,1,1,2]{3,0,2,1:T(2,128)} %copy-done.92) | copy-start | bytes 52
  556.6 23.9 %copy-start.179 = (f32[2,2,32]{2,1,0:T(2,128)S(1)}, f32[2,2,32]{2,1,0:T(2,128)}, u32[]{:S(2)}) copy-start(f32[2,2,32]{2,1,0:T(2,128)} %get-tuple-element.656) | copy-start | bytes 1540
  556.6 23.9 %copy-start.180 = (f32[2,2,32]{2,1,0:T(2,128)S(1)}, f32[2,2,32]{2,1,0:T(2,128)}, u32[]{:S(2)}) copy-start(f32[2,2,32]{2,1,0:T(2,128)} %get-tuple-element.657) | copy-start | bytes 1540
  556.6 23.1 %all-to-all-start.5 = ((f32[256,2,2,1,8]{4,1,2,3,0:T(2,128)}), f32[256,2,2,1,8]{4,1,2,3,0:T(2,128)S(1)}, u32[]{:S(2)}, u32[]{:S(2)}) async-start(f32[256,2,2,1,8]{4,1,2,3,0:T(2,128)} %copy.2505), calls=%async_computation.5 | async-start | bytes 1048576 | tf_op jit(solution)/shard_map/all_to_all | solution.py:254
  595.3 18.5 %all-to-all-start.6 = ((f32[2,2,2,128,8]{4,1,0,2,3:T(2,128)}), f32[2,2,2,128,8]{4,1,0,2,3:T(2,128)S(1)}, u32[]{:S(2)}, u32[]{:S(2)}) async-start(f32[2,2,2,128,8]{4,1,0,2,3:T(2,128)} %copy.2514), calls=%async_computation.6 | async-start | bytes 1048576 | tf_op jit(solution)/shard_map/all_to_all | solution.py:252
  633.6 18.6 %copy-start.91 = (f32[2,1,1,2]{3,0,2,1:T(2,128)S(1)}, f32[2,1,1,2]{3,0,2,1:T(2,128)}, u32[]{:S(2)}) copy-start(f32[2,1,1,2]{3,0,2,1:T(2,128)} %copy-done.90) | copy-start | bytes 52
  633.6 18.8 %copy-start.89 = (f32[2,1,1,2]{3,0,2,1:T(2,128)S(1)}, f32[2,1,1,2]{3,0,2,1:T(2,128)}, u32[]{:S(2)}) copy-start(f32[2,1,1,2]{3,0,2,1:T(2,128)} %copy-done.88) | copy-start | bytes 52
  633.6 18.9 %copy-start.177 = (f32[2,2,32]{2,1,0:T(2,128)S(1)}, f32[2,2,32]{2,1,0:T(2,128)}, u32[]{:S(2)}) copy-start(f32[2,2,32]{2,1,0:T(2,128)} %get-tuple-element.25) | copy-start | bytes 1540
  633.6 18.8 %copy-start.178 = (f32[2,2,32]{2,1,0:T(2,128)S(1)}, f32[2,2,32]{2,1,0:T(2,128)}, u32[]{:S(2)}) copy-start(f32[2,2,32]{2,1,0:T(2,128)} %get-tuple-element.26) | copy-start | bytes 1540
  (209 other events, 1927.0 us)
where the time goes:
time: 668 us; the launch traced here: 659 us
  local copies, waits for them, and re-layouts  330 us (49%)
  other arithmetic  115 us (17%)
  blocking collectives  89.7 us (13%)
  starting transfers between devices  51.4 us (8%)
  waiting for transfers between devices  48.3 us (7%)
  matrix products  16.1 us (2%)
  between operations  7.91 us (1%)
    unnamed x551, local copies, waits for them, and re-layouts  40.1 us
    all_gather x1, blocking collectives, body(): lax.all_gather(corners, 'bricks', axis=0, tiled=True)  38.2 us
    gather x18, local copies, waits for them, and re-layouts, chain_order(): pointer = jnp.take(pointer, pointer, axis=0)  35 us
    all_gather x1, blocking collectives, body(): lax.all_gather(rates, 'bricks', axis=0, tiled=True)  33.5 us
    slice x147, local copies, waits for them, and re-layouts, sorted_solve(): lax.associative_scan(compose_affine, (-f0[:, :, None], e0), reverse=True,...  31.8 us
    slice x246, local copies, waits for them, and re-layouts, sorted_solve(): summed = lax.associative_scan(compose_maps, maps, axis=0)  31.3 us
    slice x129, local copies, waits for them, and re-layouts, sorted_solve(): e1 = lax.associative_scan(compose_affine, (slope, offset), axis=0)[1]  26.4 us
    all_to_all x2, waiting for transfers between devices, solve(): lax.all_to_all(lined_jumps, 'bricks', split_axis=0, concat_axis=3, tiled=...  25.6 us
  transfers between devices with their start and end apart: 7, of which 6 were waited for; matrix products, arithmetic and copies ran while one was open for 36% of the time, Pallas kernels for 0%

commit v1 on v0

--- a/solution.py
+++ b/solution.py
@@ -9,6 +9,11 @@
 KOFF = 0.3
 BTOT = 2.0
 INFLUX = 0.1
+
+
+def gather_over(x, mesh_axis, along):
+    stack = jnp.stack([x] * lax.axis_size(mesh_axis))
+    return jnp.concatenate(lax.all_to_all(stack, mesh_axis, 0, 0), axis=along)
 
 
 def fetch(table, index):
@@ -210,7 +215,7 @@
         -1,
     )
     rate_all, corner_all = (
-        lax.all_gather(rates, "bricks", axis=0, tiled=True),
+        gather_over(rates, "bricks", 0),
         lax.all_gather(corners, "bricks", axis=0, tiled=True),
     )
     couple_all = coupling(rate_all, neighbors)

time: 668 us -> 637 us (0.954)
  blocking collectives: 89.7 us -> 56.2 us
  local copies, waits for them, and re-layouts: 330 us -> 321 us
  starting transfers between devices: 51.4 us -> 58.5 us
    all_gather x1 -> x0, blocking collectives: 33.5 us -> none  [body(): lax.all_gather(rates, 'bricks', axis=0, tiled=True)]
    all_to_all x0 -> x1, starting transfers between devices: none -> 11.5 us  [gather_over(): return jnp.concatenate(lax.all_to_all(stack, mesh_axis, 0, 0), axis=along)]
    unnamed x551 -> x510, local copies, waits for them, and re-layouts: 40.1 us -> 29.8 us
  transfers between devices with their start and end apart: 7 -> 8, of which waited for: 6 -> 6; matrix products, arithmetic and copies ran while one was open for 36% -> 42% of each run, Pallas kernels for 0% -> 0%
where the time goes in v1:
time: 637 us; the launch traced here: 626 us
  local copies, waits for them, and re-layouts  321 us (50%)
  other arithmetic  117 us (18%)
  starting transfers between devices  58.5 us (9%)
  blocking collectives  56.2 us (9%)
  waiting for transfers between devices  50.5 us (8%)
  matrix products  16.1 us (3%)
  between operations  7.5 us (1%)
    all_gather x1, blocking collectives, body(): lax.all_gather(corners, 'bricks', axis=0, tiled=True)  38.2 us
    gather x18, local copies, waits for them, and re-layouts, chain_order(): pointer = jnp.take(pointer, pointer, axis=0)  35.4 us
    slice x246, local copies, waits for them, and re-layouts, sorted_solve(): summed = lax.associative_scan(compose_maps, maps, axis=0)  31.9 us
    slice x147, local copies, waits for them, and re-layouts, sorted_solve(): lax.associative_scan(compose_affine, (-f0[:, :, None], e0), reverse=True,...  30.7 us
    unnamed x510, local copies, waits for them, and re-layouts  29.8 us
    slice x129, local copies, waits for them, and re-layouts, sorted_solve(): e1 = lax.associative_scan(compose_affine, (slope, offset), axis=0)[1]  26 us
    all_to_all x2, waiting for transfers between devices, solve(): lax.all_to_all(lined_jumps, 'bricks', split_axis=0, concat_axis=3, tiled=...  25.7 us
    all_to_all x1, blocking collectives, solve(): lax.all_to_all(lined_jumps, 'bricks', split_axis=0, concat_axis=3, tiled=...  18 us
  transfers between devices with their start and end apart: 8, of which 6 were waited for; matrix products, arithmetic and copies ran while one was open for 42% of the time, Pallas kernels for 0%

profile of v1, /device:TPU:1, one launch (start us, length us, event | category | flops | bytes accessed | tf_op | source)
XLA Modules:
  0.0 626.5 jit_solution(14922459926014036131)
XLA Ops:
  2.2 11.5 %all-to-all-start = ((f32[128,2,3,2]{2,3,1,0:T(2,128)}), f32[128,2,3,2]{2,3,1,0:T(2,128)S(1)}, u32[]{:S(2)}, u32[]{:S(2)}) async-start(f32[128,2,3,2]{2,3,1,0:T(2,128)} %stack.123), calls=%async_computation | async-start | bytes 524288 | tf_op jit(solution)/shard_map/all_to_all | solution.py:16
  20.9 4.9 divide_add_fusion
  26.4 2.7 fusion.206
  30.8 2.8 fusion.204
  34.3 2.5 fusion.202
  36.8 2.7 fusion.203
  39.5 1.9 gather_fusion.12
  44.1 1.9 gather_fusion.14
  52.0 3.2 sort.87
  55.2 3.2 sort.88
  58.3 1.9 gather_fusion.18
  60.3 2.5 gather_fusion.23
  74.5 2.4 gather_fusion.30
  77.0 3.2 sort.89
  80.1 3.2 sort.90
  83.9 2.5 gather_fusion.31
  86.4 2.5 gather_fusion.36
  101.4 3.2 sort.91
  104.6 3.2 sort.92
  110.9 2.5 gather_fusion.49
  114.4 38.2 %all_gather.3 = f32[256,3,2,4]{1,2,0,3:T(2,128)S(1)} all-gather(f32[2,3,2,4]{1,2,0,3:T(2,128)S(1)} %pad_maximum_fusion.7), channel_id=1, replica_groups=mesh['bricks'=128] {'bricks'}, dimensions={0}, use_global_device_ids=true | all-gather | bytes 24768 | tf_op jit(solution)/shard_map/all_gather | solution.py:219
  152.7 3.6 fusion.208
  158.7 2.6 gather_fusion.46
  165.9 2.6 gather_fusion.33
  171.9 2.6 copy.2422
  174.7 2.6 copy.2423
  185.6 2.1 copy.2426
  187.7 4.2 reshape.1055
  191.9 6.5 %all-to-all-start.1 = ((f32[128,1,192]{2,1,0:T(1,128)}), f32[128,1,192]{2,1,0:T(1,128)}, u32[]{:S(2)}, u32[]{:S(2)}) async-start(f32[128,1,192]{2,1,0:T(1,128)} %reshape.1055), calls=%async_computation.1 | async-start | bytes 262144 | tf_op jit(solution)/shard_map/all_to_all | solution.py:226
  307.4 3.2 reshape.1056
  310.6 1.9 bitcast_bitcast_fusion
  314.8 2.1 gather_fusion.6
  316.9 2.1 fusion.51
  319.0 2.1 gather_fusion.7
  321.1 2.3 fusion.49
  325.8 2.1 fusion.47
  327.9 2.1 gather_fusion.9
  330.0 2.1 fusion.45
  333.3 2.1 gather_fusion.10
  335.5 2.1 fusion.43
  337.6 2.1 gather_fusion.11
  343.6 4.2 reshape.1057
  347.8 10.3 %all-to-all-start.2 = ((f32[128,1,192]{2,1,0:T(1,128)}), f32[128,1,192]{2,1,0:T(1,128)S(1)}, u32[]{:S(2)}, u32[]{:S(2)}) async-start(f32[128,1,192]{2,1,0:T(1,128)} %reshape.1057), calls=%async_computation.2 | async-start | bytes 262144 | tf_op jit(solution)/shard_map/all_to_all | solution.py:230
  358.9 9.1 %all-to-all-done.2 = f32[128,1,192]{2,1,0:T(1,128)S(1)} async-done(((f32[128,1,192]{2,1,0:T(1,128)}), f32[128,1,192]{2,1,0:T(1,128)S(1)}, u32[]{:S(2)}, u32[]{:S(2)}) %all-to-all-start.2) | async-done | bytes 98336 | tf_op jit(solution)/shard_map/all_to_all | solution.py:230
  369.0 3.2 reshape.1058
  375.0 2.2 reshape.402
  377.4 2.9 copy.2442
  380.4 2.9 copy.2444
  383.9 5.0 fusion.18
  391.0 3.8 fusion.31
  397.8 4.3 all-to-all-start.3
  449.8 9.5 %all-to-all-start.4 = ((f32[256,2,2,1,8]{4,2,1,3,0:T(2,128)}), f32[256,2,2,1,8]{4,2,1,3,0:T(2,128)S(1)}, u32[]{:S(2)}, u32[]{:S(2)}) async-start(f32[256,2,2,1,8]{4,2,1,3,0:T(2,128)} %select_bitcast_fusion.2), calls=%async_computation.4 | async-start | bytes 1048576 | tf_op jit(solution)/shard_map/all_to_all | solution.py:259
  460.2 12.6 %all-to-all-done.4 = f32[256,2,2,1,8]{4,2,1,3,0:T(2,128)S(1)} async-done(((f32[256,2,2,1,8]{4,2,1,3,0:T(2,128)}), f32[256,2,2,1,8]{4,2,1,3,0:T(2,128)S(1)}, u32[]{:S(2)}, u32[]{:S(2)}) %all-to-all-start.4) | async-done | bytes 32800 | tf_op jit(solution)/shard_map/all_to_all | solution.py:259
  473.7 3.7 subtract_subtract_fusion.1
  477.4 3.2 fusion.25
  483.4 5.1 all-to-all-start.5
  498.5 3.5 all-to-all-done.5
  527.5 6.6 %all-to-all-start.6 = ((f32[256,2,2,1,8]{4,1,2,3,0:T(2,128)}), f32[256,2,2,1,8]{4,1,2,3,0:T(2,128)S(1)}, u32[]{:S(2)}, u32[]{:S(2)}) async-start(f32[256,2,2,1,8]{4,1,2,3,0:T(2,128)} %copy.2489), calls=%async_computation.6 | async-start | bytes 1048576 | tf_op jit(solution)/shard_map/all_to_all | solution.py:259
  534.5 13.1 %all-to-all-done.6 = f32[256,2,2,1,8]{4,1,2,3,0:T(2,128)S(1)} async-done(((f32[256,2,2,1,8]{4,1,2,3,0:T(2,128)}), f32[256,2,2,1,8]{4,1,2,3,0:T(2,128)S(1)}, u32[]{:S(2)}, u32[]{:S(2)}) %all-to-all-start.6) | async-done | bytes 32800 | tf_op jit(solution)/shard_map/all_to_all | solution.py:259
  548.4 3.7 subtract_subtract_fusion
  552.1 9.1 %fusion.23 = f32[2,2,32,32,32]{3,4,2,1,0:T(8,128)S(1)} fusion(f32[2,2,32,32,32]{4,2,3,1,0:T(8,128)S(1)} %subtract_subtract_fusion, f32[2,3,2,32,32]{4,3,2,1,0:T(8,128)S(1)} %copy-done.14), kind=kOutput, calls=%fused_computation.78 | convolution fusion | flops 50331648 | bytes 2686976 | tf_op jit(solution)/shard_map/psab,psijb->psija/dot_general | solution.py:82
  563.2 4.9 all-to-all-start.7
  570.0 11.5 %all-to-all-done.7 = f32[2,2,2,128,8]{4,1,0,2,3:T(2,128)S(1)} async-done(((f32[2,2,2,128,8]{4,1,0,2,3:T(2,128)}), f32[2,2,2,128,8]{4,1,0,2,3:T(2,128)S(1)}, u32[]{:S(2)}, u32[]{:S(2)}) %all-to-all-start.7) | async-done | bytes 32800 | tf_op jit(solution)/shard_map/all_to_all | solution.py:257
  601.6 18.0 %all_to_all.128 = f32[256,2,2,1,8]{4,1,2,3,0:T(2,128)S(1)} all-to-all(f32[256,2,2,1,8]{4,1,2,3,0:T(2,128)S(1)} %copy.2508), channel_id=1, replica_groups=mesh['bricks'=128] {'bricks'}, dimensions={0} | all-to-all | bytes 65536 | tf_op jit(solution)/shard_map/all_to_all | solution.py:259
  (2043 shorter events, 310.8 us)
Async XLA Ops:
  0.6 18.9 %copy-start.18 = (f32[2,32,1024]{2,1,0:T(8,128)S(1)}, f32[2,32,1024]{2,1,0:T(8,128)}, u32[]{:S(2)}) copy-start(f32[2,32,1024]{2,1,0:T(8,128)} %param.17) | copy-start | bytes 786436
  2.2 189.8 %all-to-all-start = ((f32[128,2,3,2]{2,3,1,0:T(2,128)}), f32[128,2,3,2]{2,3,1,0:T(2,128)S(1)}, u32[]{:S(2)}, u32[]{:S(2)}) async-start(f32[128,2,3,2]{2,3,1,0:T(2,128)} %stack.123), calls=%async_computation | async-start | bytes 524288 | tf_op jit(solution)/shard_map/all_to_all | solution.py:16
  58.3 112.4 %copy-start.33 = (s32[1024]{0:T(1024)}, s32[1024]{0:T(1024)S(1)}, u32[]{:S(2)}) copy-start(s32[1024]{0:T(1024)S(1)} %pad_clamp_fusion.17) | copy-start | bytes 12292
  83.9 82.0 %copy-start.32 = (s32[1024]{0:T(1024)}, s32[1024]{0:T(1024)S(1)}, u32[]{:S(2)}) copy-start(s32[1024]{0:T(1024)S(1)} %pad_clamp_fusion.9) | copy-start | bytes 12292
  108.9 49.7 %copy-start.31 = (s32[1024]{0:T(1024)}, s32[1024]{0:T(1024)S(1)}, u32[]{:S(2)}) copy-start(s32[1024]{0:T(1024)S(1)} %pad_clamp_fusion.1) | copy-start | bytes 12292
  114.0 68.4 %copy-start.35 = (pred[256]{0:T(512)(128)(4,1)}, pred[256]{0:T(512)(128)(4,1)S(1)}, u32[]{:S(2)}) copy-start(pred[256]{0:T(512)(128)(4,1)S(1)} %get-tuple-element.41) | copy-start | bytes 772
  162.4 38.6 %copy-start.170 = (s32[1024]{0:T(1024)}, s32[1024]{0:T(1024)S(1)}, u32[]{:S(2)}) copy-start(s32[1024]{0:T(1024)S(1)} %pad_clamp_fusion.26) | copy-start | bytes 12292
  191.9 113.0 %all-to-all-start.1 = ((f32[128,1,192]{2,1,0:T(1,128)}), f32[128,1,192]{2,1,0:T(1,128)}, u32[]{:S(2)}, u32[]{:S(2)}) async-start(f32[128,1,192]{2,1,0:T(1,128)} %reshape.1055), calls=%async_computation.1 | async-start | bytes 262144 | tf_op jit(solution)/shard_map/all_to_all | solution.py:226
  207.6 25.7 %copy-start.24 = (f32[256,2]{0,1:T(2,128)}, f32[256,2]{0,1:T(2,128)S(1)}, u32[]{:S(2)}) copy-start(f32[256,2]{0,1:T(2,128)S(1)} %get-tuple-element.402) | copy-start | bytes 6148
  207.6 25.7 %copy-start.26 = (f32[256,2]{0,1:T(2,128)}, f32[256,2]{0,1:T(2,128)S(1)}, u32[]{:S(2)}) copy-start(f32[256,2]{0,1:T(2,128)S(1)} %get-tuple-element.403) | copy-start | bytes 6148
  267.2 32.5 %copy-start.168 = (f32[4,2,1]{0,1,2:T(2,128)S(1)}, f32[4,2,1]{0,1,2:T(2,128)}, u32[]{:S(2)}) copy-start(f32[4,2,1]{0,1,2:T(2,128)} %copy-done.167) | copy-start | bytes 100
  267.2 33.2 %copy-start.166 = (f32[4,2,1]{0,1,2:T(2,128)S(1)}, f32[4,2,1]{0,1,2:T(2,128)}, u32[]{:S(2)}) copy-start(f32[4,2,1]{0,1,2:T(2,128)} %copy-done.165) | copy-start | bytes 100
  267.2 33.9 %copy-start.101 = (f32[2,2,1]{0,1,2:T(2,128)S(1)}, f32[2,2,1]{0,1,2:T(2,128)}, u32[]{:S(2)}) copy-start(f32[2,2,1]{0,1,2:T(2,128)} %slice.3804) | copy-start | bytes 52
  267.2 33.9 %copy-start.206 = (f32[2,2,1]{0,1,2:T(2,128)S(1)}, f32[2,2,1]{0,1,2:T(2,128)}, u32[]{:S(2)}) copy-start(f32[2,2,1]{0,1,2:T(2,128)} %slice.3808) | copy-start | bytes 52
  268.0 35.7 %copy-start.115 = (f32[2,2,1]{0,1,2:T(2,128)S(1)}, f32[2,2,1]{0,1,2:T(2,128)}, u32[]{:S(2)}) copy-start(f32[2,2,1]{0,1,2:T(2,128)} %slice.3512) | copy-start | bytes 52
  268.0 35.7 %copy-start.207 = (f32[2,2,1]{0,1,2:T(2,128)S(1)}, f32[2,2,1]{0,1,2:T(2,128)}, u32[]{:S(2)}) copy-start(f32[2,2,1]{0,1,2:T(2,128)} %slice.3516) | copy-start | bytes 52
  291.1 21.4 %copy-start.62 = (f32[64,2,1]{0,1,2:T(2,128)}, f32[64,2,1]{0,1,2:T(2,128)S(1)}, u32[]{:S(2)}) copy-start(f32[64,2,1]{0,1,2:T(2,128)S(1)} %mul.3029) | copy-start | bytes 1540
  293.5 19.0 %copy-start.141 = (f32[2,2,1]{0,1,2:T(2,128)}, f32[2,2,1]{0,1,2:T(2,128)S(1)}, u32[]{:S(2)}) copy-start(f32[2,2,1]{0,1,2:T(2,128)S(1)} %slice.3220) | copy-start | bytes 52
  302.1 81.7 %copy-start.91 = (f32[2,1,1,2]{3,0,2,1:T(2,128)}, f32[2,1,1,2]{3,0,2,1:T(2,128)S(1)}, u32[]{:S(2)}) copy-start(f32[2,1,1,2]{3,0,2,1:T(2,128)S(1)} %copy.2441) | copy-start | bytes 52
  302.2 81.6 %copy-start.93 = (f32[2,1,1,2]{3,0,2,1:T(2,128)}, f32[2,1,1,2]{3,0,2,1:T(2,128)S(1)}, u32[]{:S(2)}) copy-start(f32[2,1,1,2]{3,0,2,1:T(2,128)S(1)} %copy.2443) | copy-start | bytes 52
  302.3 86.7 %copy-start.95 = (f32[2,1,1,2]{3,0,2,1:T(2,128)}, f32[2,1,1,2]{3,0,2,1:T(2,128)S(1)}, u32[]{:S(2)}) copy-start(f32[2,1,1,2]{3,0,2,1:T(2,128)S(1)} %copy.2439) | copy-start | bytes 52
  302.4 86.6 %copy-start.98 = (f32[2,1,1,2]{3,0,2,1:T(2,128)}, f32[2,1,1,2]{3,0,2,1:T(2,128)S(1)}, u32[]{:S(2)}) copy-start(f32[2,1,1,2]{3,0,2,1:T(2,128)S(1)} %copy.2440) | copy-start | bytes 52
  347.8 20.2 %all-to-all-start.2 = ((f32[128,1,192]{2,1,0:T(1,128)}), f32[128,1,192]{2,1,0:T(1,128)S(1)}, u32[]{:S(2)}, u32[]{:S(2)}) async-start(f32[128,1,192]{2,1,0:T(1,128)} %reshape.1057), calls=%async_computation.2 | async-start | bytes 262144 | tf_op jit(solution)/shard_map/all_to_all | solution.py:230
  395.0 18.6 %copy-start.88 = (f32[256,2,1]{0,1,2:T(2,128)S(1)}, f32[256,2,1]{0,1,2:T(2,128)}, u32[]{:S(2)}) copy-start(f32[256,2,1]{0,1,2:T(2,128)} %copy-done.87) | copy-start | bytes 6148
  397.8 17.9 %all-to-all-start.3 = ((f32[2,2,2,128,8]{4,1,0,2,3:T(2,128)}), f32[2,2,2,128,8]{4,1,0,2,3:T(2,128)S(1)}, u32[]{:S(2)}, u32[]{:S(2)}) async-start(f32[2,2,2,128,8]{4,1,0,2,3:T(2,128)} %copy.2459), calls=%async_computation.3 | async-start | bytes 1048576 | tf_op jit(solution)/shard_map/all_to_all | solution.py:257
  416.4 25.9 %copy-start.142 = (f32[2,2,1]{0,1,2:T(2,128)S(1)}, f32[2,2,1]{0,1,2:T(2,128)}, u32[]{:S(2)}) copy-start(f32[2,2,1]{0,1,2:T(2,128)} %copy-done.141) | copy-start | bytes 52
  417.7 23.4 %copy-start.148 = (f32[4,2,1]{0,1,2:T(2,128)S(1)}, f32[4,2,1]{0,1,2:T(2,128)}, u32[]{:S(2)}) copy-start(f32[4,2,1]{0,1,2:T(2,128)} %copy-done.147) | copy-start | bytes 100
  417.7 24.6 %copy-start.246 = (f32[2]{0:T(128)S(1)}, f32[2]{0:T(128)}, u32[]{:S(2)}) copy-start(f32[2]{0:T(128)} %slice_reduce_fusion.29) | copy-start | bytes 28
  417.7 24.8 %copy-start.245 = (f32[2]{0:T(128)S(1)}, f32[2]{0:T(128)}, u32[]{:S(2)}) copy-start(f32[2]{0:T(128)} %slice_reduce_fusion.30) | copy-start | bytes 28
  417.7 25.3 %copy-start.217 = (f32[3,2,1]{0,1,2:T(2,128)S(1)}, f32[3,2,1]{0,1,2:T(2,128)}, u32[]{:S(2)}) copy-start(f32[3,2,1]{0,1,2:T(2,128)} %slice.3211) | copy-start | bytes 76
  417.7 25.6 %copy-start.215 = (f32[7,2,1]{0,1,2:T(2,128)S(1)}, f32[7,2,1]{0,1,2:T(2,128)}, u32[]{:S(2)}) copy-start(f32[7,2,1]{0,1,2:T(2,128)} %slice.3204) | copy-start | bytes 172
  417.7 26.2 %copy-start.213 = (f32[15,2,1]{0,1,2:T(2,128)S(1)}, f32[15,2,1]{0,1,2:T(2,128)}, u32[]{:S(2)}) copy-start(f32[15,2,1]{0,1,2:T(2,128)} %slice.3197) | copy-start | bytes 364
  417.7 26.4 %copy-start.211 = (f32[31,2,1]{0,1,2:T(2,128)S(1)}, f32[31,2,1]{0,1,2:T(2,128)}, u32[]{:S(2)}) copy-start(f32[31,2,1]{0,1,2:T(2,128)} %slice.3190) | copy-start | bytes 748
  417.7 27.2 %copy-start.210 = (f32[63,2,1]{0,1,2:T(2,128)S(1)}, f32[63,2,1]{0,1,2:T(2,128)}, u32[]{:S(2)}) copy-start(f32[63,2,1]{0,1,2:T(2,128)} %slice.3183) | copy-start | bytes 1516
  417.7 27.7 %copy-start.209 = (f32[127,2,1]{0,1,2:T(2,128)S(1)}, f32[127,2,1]{0,1,2:T(2,128)}, u32[]{:S(2)}) copy-start(f32[127,2,1]{0,1,2:T(2,128)} %slice.3172) | copy-start | bytes 3052
  417.7 29.0 %copy-start.183 = (f32[256,2]{0,1:T(2,128)S(1)}, f32[256,2]{0,1:T(2,128)}, u32[]{:S(2)}) copy-start(f32[256,2]{0,1:T(2,128)} %get-tuple-element.248) | copy-start | bytes 6148
  417.8 29.0 %copy-start.237 = (pred[256]{0:T(512)(128)(4,1)S(1)}, pred[256]{0:T(512)(128)(4,1)}, u32[]{:S(2)}) copy-start(pred[256]{0:T(512)(128)(4,1)} %select_compare_fusion.4) | copy-start | bytes 772
  417.8 29.0 %copy-start.236 = (pred[256]{0:T(512)(128)(4,1)S(1)}, pred[256]{0:T(512)(128)(4,1)}, u32[]{:S(2)}) copy-start(pred[256]{0:T(512)(128)(4,1)} %get-tuple-element.244) | copy-start | bytes 772
  429.4 19.1 %copy-start.240 = (pred[256]{0:T(512)(128)(4,1)S(1)}, pred[256]{0:T(512)(128)(4,1)}, u32[]{:S(2)}) copy-start(pred[256]{0:T(512)(128)(4,1)} %compare_and_fusion.4) | copy-start | bytes 772
  449.8 23.6 %copy-start.202 = (f32[2,1,1,2]{3,0,2,1:T(2,128)S(1)}, f32[2,1,1,2]{3,0,2,1:T(2,128)}, u32[]{:S(2)}) copy-start(f32[2,1,1,2]{3,0,2,1:T(2,128)} %copy.2438) | copy-start | bytes 52
  449.8 23.8 %copy-start.200 = (f32[2,1,1,2]{3,0,2,1:T(2,128)S(1)}, f32[2,1,1,2]{3,0,2,1:T(2,128)}, u32[]{:S(2)}) copy-start(f32[2,1,1,2]{3,0,2,1:T(2,128)} %copy.2417) | copy-start | bytes 52
  449.8 23.9 %copy-start.96 = (f32[2,1,1,2]{3,0,2,1:T(2,128)S(1)}, f32[2,1,1,2]{3,0,2,1:T(2,128)}, u32[]{:S(2)}) copy-start(f32[2,1,1,2]{3,0,2,1:T(2,128)} %copy-done.95) | copy-start | bytes 52
  449.8 23.9 %copy-start.99 = (f32[2,1,1,2]{3,0,2,1:T(2,128)S(1)}, f32[2,1,1,2]{3,0,2,1:T(2,128)}, u32[]{:S(2)}) copy-start(f32[2,1,1,2]{3,0,2,1:T(2,128)} %copy-done.98) | copy-start | bytes 52
  449.8 23.9 %copy-start.177 = (f32[2,2,32]{2,1,0:T(2,128)S(1)}, f32[2,2,32]{2,1,0:T(2,128)}, u32[]{:S(2)}) copy-start(f32[2,2,32]{2,1,0:T(2,128)} %get-tuple-element.29) | copy-start | bytes 1540
  449.8 23.9 %copy-start.178 = (f32[2,2,32]{2,1,0:T(2,128)S(1)}, f32[2,2,32]{2,1,0:T(2,128)}, u32[]{:S(2)}) copy-start(f32[2,2,32]{2,1,0:T(2,128)} %get-tuple-element.30) | copy-start | bytes 1540
  449.8 23.9 %copy-start.197 = (f32[2,2]{1,0:T(2,128)S(1)}, f32[2,2]{1,0:T(2,128)}, u32[]{:S(2)}) copy-start(f32[2,2]{1,0:T(2,128)} %get-tuple-element.37) | copy-start | bytes 52
  449.8 23.9 %copy-start.227 = (pred[32]{0:T(512)(128)(4,1)S(1)}, pred[32]{0:T(512)(128)(4,1)}, u32[]{:S(2)}) copy-start(pred[32]{0:T(512)(128)(4,1)} %get-tuple-element.654) | copy-start | bytes 100
  449.8 23.9 %copy-start.229 = (pred[32]{0:T(512)(128)(4,1)S(1)}, pred[32]{0:T(512)(128)(4,1)}, u32[]{:S(2)}) copy-start(pred[32]{0:T(512)(128)(4,1)} %get-tuple-element.655) | copy-start | bytes 100
  449.8 23.0 %all-to-all-start.4 = ((f32[256,2,2,1,8]{4,2,1,3,0:T(2,128)}), f32[256,2,2,1,8]{4,2,1,3,0:T(2,128)S(1)}, u32[]{:S(2)}, u32[]{:S(2)}) async-start(f32[256,2,2,1,8]{4,2,1,3,0:T(2,128)} %select_bitcast_fusion.2), calls=%async_computation.4 | async-start | bytes 1048576 | tf_op jit(solution)/shard_map/all_to_all | solution.py:259
  483.4 18.6 %all-to-all-start.5 = ((f32[2,2,2,128,8]{4,1,0,2,3:T(2,128)}), f32[2,2,2,128,8]{4,1,0,2,3:T(2,128)S(1)}, u32[]{:S(2)}, u32[]{:S(2)}) async-start(f32[2,2,2,128,8]{4,1,0,2,3:T(2,128)} %copy.2479), calls=%async_computation.5 | async-start | bytes 1048576 | tf_op jit(solution)/shard_map/all_to_all | solution.py:257
  502.8 18.8 %copy-start.212 = (f32[31,2,1]{0,1,2:T(2,128)S(1)}, f32[31,2,1]{0,1,2:T(2,128)}, u32[]{:S(2)}) copy-start(f32[31,2,1]{0,1,2:T(2,128)} %slice.3482) | copy-start | bytes 748
  504.3 20.0 %copy-start.182 = (f32[256,2]{0,1:T(2,128)S(1)}, f32[256,2]{0,1:T(2,128)}, u32[]{:S(2)}) copy-start(f32[256,2]{0,1:T(2,128)} %get-tuple-element.146) | copy-start | bytes 6148
  504.3 19.9 %copy-start.235 = (pred[256]{0:T(512)(128)(4,1)S(1)}, pred[256]{0:T(512)(128)(4,1)}, u32[]{:S(2)}) copy-start(pred[256]{0:T(512)(128)(4,1)} %select_compare_fusion.2) | copy-start | bytes 772
  504.3 20.0 %copy-start.234 = (pred[256]{0:T(512)(128)(4,1)S(1)}, pred[256]{0:T(512)(128)(4,1)}, u32[]{:S(2)}) copy-start(pred[256]{0:T(512)(128)(4,1)} %get-tuple-element.142) | copy-start | bytes 772
  527.5 20.7 %copy-start.100 = (f32[2,1,1,2]{3,0,2,1:T(2,128)S(1)}, f32[2,1,1,2]{3,0,2,1:T(2,128)}, u32[]{:S(2)}) copy-start(f32[2,1,1,2]{3,0,2,1:T(2,128)} %copy-done.98) | copy-start | bytes 52
  527.5 20.8 %copy-start.97 = (f32[2,1,1,2]{3,0,2,1:T(2,128)S(1)}, f32[2,1,1,2]{3,0,2,1:T(2,128)}, u32[]{:S(2)}) copy-start(f32[2,1,1,2]{3,0,2,1:T(2,128)} %copy-done.95) | copy-start | bytes 52
  527.5 20.9 %copy-start.175 = (f32[2,2,32]{2,1,0:T(2,128)S(1)}, f32[2,2,32]{2,1,0:T(2,128)}, u32[]{:S(2)}) copy-start(f32[2,2,32]{2,1,0:T(2,128)} %get-tuple-element.656) | copy-start | bytes 1540
  527.5 20.9 %copy-start.176 = (f32[2,2,32]{2,1,0:T(2,128)S(1)}, f32[2,2,32]{2,1,0:T(2,128)}, u32[]{:S(2)}) copy-start(f32[2,2,32]{2,1,0:T(2,128)} %get-tuple-element.657) | copy-start | bytes 1540
  527.5 20.1 %all-to-all-start.6 = ((f32[256,2,2,1,8]{4,1,2,3,0:T(2,128)}), f32[256,2,2,1,8]{4,1,2,3,0:T(2,128)S(1)}, u32[]{:S(2)}, u32[]{:S(2)}) async-start(f32[256,2,2,1,8]{4,1,2,3,0:T(2,128)} %copy.2489), calls=%async_computation.6 | async-start | bytes 1048576 | tf_op jit(solution)/shard_map/all_to_all | solution.py:259
  563.2 18.4 %all-to-all-start.7 = ((f32[2,2,2,128,8]{4,1,0,2,3:T(2,128)}), f32[2,2,2,128,8]{4,1,0,2,3:T(2,128)S(1)}, u32[]{:S(2)}, u32[]{:S(2)}) async-start(f32[2,2,2,128,8]{4,1,0,2,3:T(2,128)} %copy.2498), calls=%async_computation.7 | async-start | bytes 1048576 | tf_op jit(solution)/shard_map/all_to_all | solution.py:257
  601.6 18.6 %copy-start.94 = (f32[2,1,1,2]{3,0,2,1:T(2,128)S(1)}, f32[2,1,1,2]{3,0,2,1:T(2,128)}, u32[]{:S(2)}) copy-start(f32[2,1,1,2]{3,0,2,1:T(2,128)} %copy-done.93) | copy-start | bytes 52
  601.6 18.8 %copy-start.92 = (f32[2,1,1,2]{3,0,2,1:T(2,128)S(1)}, f32[2,1,1,2]{3,0,2,1:T(2,128)}, u32[]{:S(2)}) copy-start(f32[2,1,1,2]{3,0,2,1:T(2,128)} %copy-done.91) | copy-start | bytes 52
  601.6 18.9 %copy-start.173 = (f32[2,2,32]{2,1,0:T(2,128)S(1)}, f32[2,2,32]{2,1,0:T(2,128)}, u32[]{:S(2)}) copy-start(f32[2,2,32]{2,1,0:T(2,128)} %get-tuple-element.25) | copy-start | bytes 1540
  601.6 18.8 %copy-start.174 = (f32[2,2,32]{2,1,0:T(2,128)S(1)}, f32[2,2,32]{2,1,0:T(2,128)}, u32[]{:S(2)}) copy-start(f32[2,2,32]{2,1,0:T(2,128)} %get-tuple-element.26) | copy-start | bytes 1540
  (191 other events, 1636.9 us)
